TPU v7x, 128 devices: a whole 4x4x4 slice. The times are simulated.
128 devices in a mesh: dp: 16 (over x, y), expert: 8 (over z, core).
Axes of the slice: x: 4, y: 4, z: 4, core: 2. Of those that a mesh axis runs over, the one named last changes fastest.
Arguments:
- tokens: bfloat16 [2048, 4096], P('dp', 'expert'), may hold values from -6 to 6
- output_gradient: bfloat16 [2048, 4096], P('dp', 'expert'), may hold values from -6 to 6
- routing: int32 [2048, 2], P('dp'), may hold values from 0 to 7, all different within a row; in each aligned block of 128 rows (0 to 127, 128 to 255, ...) at most 96 rows name the same one
- router_gate_values: float32 [2048, 2], P('dp'), may hold values from 0.1 to 0.9
- gate_weight: bfloat16 [8, 7168, 4096], P('expert', 'dp'), may hold values from -0.09375 to 0.09375
- up_weight: bfloat16 [8, 7168, 4096], P('expert', 'dp'), may hold values from -0.09375 to 0.09375
- down_weight: bfloat16 [8, 7168, 4096], P('expert', 'dp'), may hold values from -0.0625 to 0.0625
- adapter_lower_gate: bfloat16 [8, 16, 4096], P('expert'), may hold values from -0.09375 to 0.09375
- adapter_upper_gate: bfloat16 [8, 7168, 16], P('expert', 'dp'), may hold values from -0.375 to 0.375
- adapter_lower_up: bfloat16 [8, 16, 4096], P('expert'), may hold values from -0.09375 to 0.09375
- adapter_upper_up: bfloat16 [8, 7168, 16], P('expert', 'dp'), may hold values from -0.375 to 0.375
- adapter_lower_down: bfloat16 [8, 16, 7168], P('expert', None, 'dp'), may hold values from -0.0625 to 0.0625
- adapter_upper_down: bfloat16 [8, 4096, 16], P('expert'), may hold values from -0.375 to 0.375
Outputs:
- grad_x: bfloat16 [2048, 4096], P('dp', 'expert')
- grad_lora_a_gate: float32 [8, 16, 4096], P('expert')
- grad_lora_b_gate: float32 [8, 7168, 16], P('expert', 'dp')
- grad_lora_a_up: float32 [8, 16, 4096], P('expert')
- grad_lora_b_up: float32 [8, 7168, 16], P('expert', 'dp')
- grad_lora_a_down: float32 [8, 16, 7168], P('expert', None, 'dp')
- grad_lora_b_down: float32 [8, 4096, 16], P('expert')
Inputs may be any that keep to these rules, and one draw needn't show every extreme that they name: `routing`: each row names two different experts. In the rows of one dp shard (aligned blocks of 128 rows) no expert is named by more than 96 rows, and in some blocks one expert is named by exactly 96 rows.
All inputs are finite; a program needn't handle non-finite values.
Results may differ from a plain program's by a relative error of at most 0.015.
Values may be sent and summed in bfloat16 or wider, within the bound.
A program may use at most 256 MiB of HBM per device.

v0:
```python
import jax
import jax.numpy as jnp
from jax import lax
from jax.sharding import PartitionSpec as P

ADAPTER_SCALE = 2.0


def contract_pair(left, right, left_axis, right_axis):
    return lax.dot_general(
        left, right, (((left_axis,), (right_axis,)), ((), ())), preferred_element_type=jnp.float32
    )


def slot_numbers(route_rows, experts):
    picked = (route_rows[:, :, None] == jnp.arange(experts, dtype=jnp.int32)[None, None, :]).astype(
        jnp.int32
    )
    per_token = jnp.sum(picked, axis=1)
    earlier = jnp.cumsum(per_token, axis=0) - per_token
    return jnp.sum(earlier[:, None, :] * picked, axis=2)


def slot_sources(route_rows, positions, experts, capacity):
    tokens_here, choose = route_rows.shape
    target = (route_rows * capacity + positions).reshape(-1)
    owners = jnp.repeat(jnp.arange(tokens_here, dtype=jnp.int32), choose)
    member_ids = jnp.tile(jnp.arange(choose, dtype=jnp.int32), tokens_here)
    source = jnp.full((experts * capacity,), tokens_here, jnp.int32).at[target].set(owners)
    member = jnp.zeros((experts * capacity,), jnp.int32).at[target].set(member_ids)
    return (source, member)


def rows_backward_pass(input_rows, output_gradient_rows, params):
    (
        gate_weight,
        up_weight,
        down_weight,
        a_gate,
        gate_adapter_upper,
        a_up,
        up_adapter_upper,
        down_adapter_lower,
        b_down,
    ) = params
    gate_projected_lower = contract_pair(a_gate, input_rows, 1, 1).astype(jnp.bfloat16)
    up_projected_lower = contract_pair(a_up, input_rows, 1, 1).astype(jnp.bfloat16)
    gate_preactivation = contract_pair(
        gate_weight, input_rows, 1, 1
    ) + ADAPTER_SCALE * contract_pair(gate_adapter_upper, gate_projected_lower, 1, 0)
    up_preactivation = contract_pair(up_weight, input_rows, 1, 1) + ADAPTER_SCALE * contract_pair(
        up_adapter_upper, up_projected_lower, 1, 0
    )
    sigmoid_gate = jax.nn.sigmoid(gate_preactivation)
    silu_gate = gate_preactivation * sigmoid_gate
    hidden_units = (silu_gate * up_preactivation).astype(jnp.bfloat16)
    down_projected_lower = contract_pair(b_down, output_gradient_rows, 0, 1).astype(jnp.bfloat16)
    hidden_gradient = contract_pair(
        down_weight, output_gradient_rows, 1, 1
    ) + ADAPTER_SCALE * contract_pair(down_adapter_lower, down_projected_lower, 0, 0)
    gate_gradient = (
        hidden_gradient
        * up_preactivation
        * sigmoid_gate
        * (1.0 + gate_preactivation * (1.0 - sigmoid_gate))
    ).astype(jnp.bfloat16)
    up_gradient = (hidden_gradient * silu_gate).astype(jnp.bfloat16)
    gate_partial = contract_pair(gate_adapter_upper, gate_gradient, 0, 0).astype(jnp.bfloat16)
    up_partial = contract_pair(up_adapter_upper, up_gradient, 0, 0).astype(jnp.bfloat16)
    down_partial = contract_pair(down_adapter_lower, hidden_units, 1, 0).astype(jnp.bfloat16)
    paired_partials = jnp.concatenate([gate_partial, up_partial], 0)
    paired_factors = jnp.concatenate([a_gate, a_up], 0)
    gradient_rows_out = (
        contract_pair(gate_gradient, gate_weight, 0, 0)
        + contract_pair(up_gradient, up_weight, 0, 0)
        + ADAPTER_SCALE * contract_pair(paired_partials, paired_factors, 0, 0)
    )
    shared_slice = (
        ADAPTER_SCALE * contract_pair(gate_partial, input_rows, 1, 0),
        ADAPTER_SCALE * contract_pair(up_partial, input_rows, 1, 0),
        ADAPTER_SCALE * contract_pair(output_gradient_rows, down_partial, 0, 1),
    )
    owned_slice = (
        ADAPTER_SCALE * contract_pair(gate_gradient, gate_projected_lower, 1, 1),
        ADAPTER_SCALE * contract_pair(up_gradient, up_projected_lower, 1, 1),
        ADAPTER_SCALE * contract_pair(down_projected_lower, hidden_units, 1, 1),
    )
    return (gradient_rows_out, shared_slice, owned_slice)


def local(
    tokens,
    output_gradient,
    routing,
    router_gate_values,
    gate_weight,
    up_weight,
    down_weight,
    adapter_lower_gate,
    adapter_upper_gate,
    adapter_lower_up,
    adapter_upper_up,
    adapter_lower_down,
    adapter_upper_down,
):
    experts = lax.axis_size("expert")
    shards = lax.axis_size("dp")
    tok_local, feat_local = tokens.shape
    choose = routing.shape[1]
    complete_width = feat_local * experts
    capacity = min(tok_local, 6 * tok_local // experts)
    hidden_units_local = gate_weight.shape[1]
    adapter_rank = adapter_lower_gate.shape[1]
    params = (
        gate_weight[0],
        up_weight[0],
        down_weight[0],
        adapter_lower_gate[0],
        adapter_upper_gate[0],
        adapter_lower_up[0],
        adapter_upper_up[0],
        adapter_lower_down[0],
        adapter_upper_down[0],
    )
    positions = slot_numbers(routing, experts)
    zero_row = jnp.zeros((1, feat_local), jnp.bfloat16)
    initial = (
        jnp.zeros((shards * capacity, complete_width), jnp.float32),
        (
            jnp.zeros((adapter_rank, complete_width), jnp.float32),
            jnp.zeros((adapter_rank, complete_width), jnp.float32),
            jnp.zeros((complete_width, adapter_rank), jnp.float32),
        ),
        (
            jnp.zeros((hidden_units_local, adapter_rank), jnp.float32),
            jnp.zeros((hidden_units_local, adapter_rank), jnp.float32),
            jnp.zeros((adapter_rank, hidden_units_local), jnp.float32),
        ),
    )
    source, member = slot_sources(routing, positions, experts, capacity)
    clamped = jnp.minimum(source, tok_local - 1)
    slot_gate = jnp.where(
        source < tok_local, router_gate_values.reshape(-1)[clamped * choose + member], 0.0
    )
    send_x = jnp.concatenate([tokens, zero_row], 0)[source].reshape(experts, capacity, feat_local)
    send_dy = (
        (
            slot_gate[:, None]
            * jnp.concatenate([output_gradient, zero_row], 0)[source].astype(jnp.float32)
        )
        .astype(jnp.bfloat16)
        .reshape(experts, capacity, feat_local)
    )
    recv_x, recv_dy = (
        lax.all_to_all(send_x, "expert", split_axis=0, concat_axis=2, tiled=True),
        lax.all_to_all(send_dy, "expert", split_axis=0, concat_axis=2, tiled=True),
    )
    gradient_rows_out, shared_slice, owned_slice = rows_backward_pass(
        lax.all_gather(recv_x[0], "dp", axis=0, tiled=True),
        lax.all_gather(recv_dy[0], "dp", axis=0, tiled=True),
        params,
    )
    rows_part = gradient_rows_out
    totals = (
        rows_part,
        jax.tree.map(jnp.add, initial[1], shared_slice),
        jax.tree.map(jnp.add, initial[2], owned_slice),
    )
    rows_part, shared_slice, owned_slice = totals
    summed = lax.psum_scatter(
        rows_part.astype(jnp.bfloat16), "dp", scatter_dimension=0, tiled=True
    ).astype(jnp.float32)
    returned_rows = lax.all_to_all(
        summed.reshape(capacity, experts, feat_local).astype(jnp.bfloat16),
        "expert",
        split_axis=1,
        concat_axis=1,
        tiled=True,
    ).astype(jnp.float32)
    lookup = positions * experts + routing
    grad_x = jnp.sum(returned_rows.reshape(capacity * experts, feat_local)[lookup], axis=1).astype(
        jnp.bfloat16
    )
    grad_a_gate, grad_a_up, grad_b_down = (
        lax.psum(shared_slice[0].astype(jnp.bfloat16), "dp").astype(jnp.float32),
        lax.psum(shared_slice[1].astype(jnp.bfloat16), "dp").astype(jnp.float32),
        lax.psum(shared_slice[2].astype(jnp.bfloat16), "dp").astype(jnp.float32),
    )
    return (
        grad_x,
        grad_a_gate[None],
        owned_slice[0][None],
        grad_a_up[None],
        owned_slice[1][None],
        owned_slice[2][None],
        grad_b_down[None],
    )


def solution(mesh):
    return jax.shard_map(
        local,
        mesh=mesh,
        in_specs=(
            P("dp", "expert"),
            P("dp", "expert"),
            P("dp", None),
            P("dp", None),
            P("expert", "dp", None),
            P("expert", "dp", None),
            P("expert", "dp", None),
            P("expert", None, None),
            P("expert", "dp", None),
            P("expert", None, None),
            P("expert", "dp", None),
            P("expert", None, "dp"),
            P("expert", None, None),
        ),
        out_specs=(
            P("dp", "expert"),
            P("expert", None, None),
            P("expert", "dp", None),
            P("expert", None, None),
            P("expert", "dp", None),
            P("expert", None, "dp"),
            P("expert", None, None),
        ),
        check_vma=False,
    )
```

profile of v0, /device:TPU:0, one launch (start us, length us, event | category | flops | bytes accessed | tf_op | source)
XLA Modules:
  0.0 502.2 jit_solution(6191401442853904213)
XLA Ops:
  7.2 0.0 all-gather.5.cloned.1.call-start
  7.2 0.7 convert_reduce_fusion
  7.9 0.1 copy.42
  8.1 0.2 reduce_window_sum.11
  8.3 0.7 select_reduce_fusion
  9.0 0.7 compare_select_fusion.3
  9.7 0.1 copy.45
  9.8 0.1 reshape.84
  10.0 0.1 reshape.137
  10.1 0.1 reshape.129
  10.3 1.4 scatter_custom_fusion.1
  11.7 1.4 scatter_custom_fusion
  13.1 0.9 concatenate.13
  14.0 2.7 gather_fusion.2
  16.7 18.4 %all_to_all.35 = bf16[8,96,512]{2,1,0:T(8,128)(2,1)S(1)} all-to-all(bf16[8,96,512]{2,1,0:T(8,128)(2,1)S(1)} %bitcast.118), channel_id=1, replica_groups=mesh['dp'=16,'expert'=8] {'expert'}, dimensions={0} | all-to-all | bytes 1572864 | tf_op jit(solution)/shard_map/all_to_all | solution.py:155
  35.2 1.0 copy.54
  36.2 0.0 all-gather.3.cloned.1.call-start
  36.2 0.1 copy.46
  36.3 0.1 reshape.86
  36.5 5.0 gather_fusion
  41.5 0.1 mul.106
  41.6 2.7 gather_fusion.1
  44.3 0.2 fusion.23
  44.5 15.7 %all_to_all.36 = bf16[8,96,512]{2,1,0:T(8,128)(2,1)S(1)} all-to-all(bf16[8,96,512]{2,1,0:T(8,128)(2,1)S(1)} %fusion.23), channel_id=1, replica_groups=mesh['dp'=16,'expert'=8] {'expert'}, dimensions={0} | all-to-all | bytes 1572864 | tf_op jit(solution)/shard_map/all_to_all | solution.py:156
  60.2 1.0 copy.53
  61.2 0.6 reduce-scatter.2.cloned.1.call-start
  61.8 63.9 %all-gather.5.cloned.1.call-done = bf16[1536,4096]{1,0:T(8,128)(2,1)} async-done(((bf16[96,4096]{1,0:T(8,128)(2,1)}), bf16[1536,4096]{1,0:T(8,128)(2,1)}) %all-gather.5.cloned.1.call-update) | async-done | bytes 12582928 | tf_op jit(solution)/shard_map/all_gather | solution.py:159
  125.7 8.1 %convolution_convert_fusion.3 = bf16[1536,16]{0,1:T(8,128)(2,1)S(1)} fusion(bf16[1536,4096]{1,0:T(8,128)(2,1)} %all-gather.5.cloned.1.call-done, bf16[1,16,4096]{2,1,0:T(8,128)(2,1)S(1)} %copy-done.5), kind=kOutput, calls=%fused_computation.43 | convolution fusion | flops 201351168 | bytes 12763136 | tf_op jit(solution)/shard_map/dot_general | solution.py:10
  133.8 0.1 copy-done.2
  133.9 8.0 %fusion.8 = f32[1536,448]{0,1:T(8,128)S(1)} fusion(bf16[1536,4096]{1,0:T(8,128)(2,1)S(1)} %copy-done.2, bf16[1,448,4096]{2,1,0:T(8,128)(2,1)} %param.17), kind=kOutput, calls=%fused_computation.18 | convolution fusion | flops 5637144576 | bytes 19005440 | tf_op jit(solution)/shard_map/dot_general | solution.py:10
  141.8 2.1 fusion.21
  144.0 73.6 %all-gather.3.cloned.1.call-done = bf16[1536,4096]{1,0:T(8,128)(2,1)} async-done(((bf16[96,4096]{1,0:T(8,128)(2,1)}), bf16[1536,4096]{1,0:T(8,128)(2,1)}) %all-gather.3.cloned.1.call-update) | async-done | bytes 12582928 | tf_op jit(solution)/shard_map/all_gather | solution.py:160
  217.5 8.1 %convolution_convert_fusion.5 = bf16[1536,16]{0,1:T(8,128)(2,1)S(1)} fusion(bf16[1536,4096]{1,0:T(8,128)(2,1)} %all-gather.3.cloned.1.call-done, bf16[1,4096,16]{1,2,0:T(8,128)(2,1)S(1)} %copy-done), kind=kOutput, calls=%fused_computation.45 | convolution fusion | flops 201351168 | bytes 12763136 | tf_op jit(solution)/shard_map/dot_general | solution.py:10
  225.6 9.3 %fusion.14 = f32[1536,448]{0,1:T(8,128)S(1)} fusion(bf16[1536,4096]{1,0:T(8,128)(2,1)} %all-gather.3.cloned.1.call-done, bf16[1,448,4096]{2,1,0:T(8,128)(2,1)S(1)} %copy-done.12), kind=kOutput, calls=%fused_computation.24 | convolution fusion | flops 5637144576 | bytes 19005440 | tf_op jit(solution)/shard_map/dot_general | solution.py:10
  234.9 0.6 fusion.19
  235.5 0.3 copy-done.6
  235.8 3.3 convolution_convert_fusion.4
  239.2 5.9 %fusion.12 = f32[1536,448]{0,1:T(8,128)S(1)} fusion(bf16[1536,4096]{1,0:T(8,128)(2,1)S(1)} %bitcast.115, bf16[1,448,4096]{2,1,0:T(8,128)(2,1)S(1)} %copy-done.13), kind=kOutput, calls=%fused_computation.22 | convolution fusion | flops 5637144576 | bytes 19005440 | tf_op jit(solution)/shard_map/dot_general | solution.py:10
  245.1 2.7 multiply_convert_fusion
  247.9 0.3 convolution_convert_fusion.1
  248.1 12.0 %fusion.10 = f32[1536,4096]{1,0:T(8,128)} fusion(bf16[448,1536]{1,0:T(8,128)(2,1)S(1)} %get-tuple-element.12, bf16[1,448,4096]{2,1,0:T(8,128)(2,1)S(1)} %copy-done.13), kind=kOutput, calls=%fused_computation.20 | convolution fusion | flops 5637144576 | bytes 30212096 | tf_op jit(solution)/shard_map/dot_general | solution.py:10
  260.1 0.3 convolution_convert_fusion.2
  260.4 11.7 %fusion.6 = f32[1536,4096]{1,0:T(8,128)} fusion(bf16[448,1536]{1,0:T(8,128)(2,1)S(1)} %get-tuple-element.11, bf16[1,448,4096]{2,1,0:T(8,128)(2,1)S(1)} %copy-done.14), kind=kOutput, calls=%fused_computation.16 | convolution fusion | flops 5637144576 | bytes 30212096 | tf_op jit(solution)/shard_map/dot_general | solution.py:10
  272.1 21.9 %add_convert_fusion = bf16[1536,4096]{1,0:T(8,128)(2,1)} fusion(f32[1536,4096]{1,0:T(8,128)} %fusion.6, f32[1536,4096]{1,0:T(8,128)} %fusion.10, bf16[16,4096]{1,0:T(8,128)(2,1)S(1)} %bitcast.128, bf16[16,4096]{1,0:T(8,128)(2,1)S(1)} %bitcast.127, bf16[16,1536]{1,0:T(8,128)(2,1)S(1)} %bitcast.126, bf16[16,1536]{1,0:T(8,128)(2,1)S(1)} %bitcast.125), kind=kOutput, calls=%fused_computation.6 | convolution fusion | flops 428539904 | bytes 63275008 | tf_op jit(solution)/shard_map/dot_general | solution.py:10
  294.0 0.1 copy.51
  294.1 0.1 reshape.119
  294.3 7.0 %fusion.4 = bf16[1,16,4096]{2,1,0:T(8,128)(2,1)} fusion(bf16[1536,16]{0,1:T(8,128)(2,1)S(1)} %convolution_convert_fusion.1, bf16[1536,4096]{1,0:T(8,128)(2,1)} %all-gather.5.cloned.1.call-done), kind=kOutput, calls=%fused_computation.14 | convolution fusion | flops 201457664 | bytes 12763136 | tf_op jit(solution)/shard_map/dot_general | solution.py:10
  301.2 8.2 %fusion.3 = bf16[1,4096,16]{1,2,0:T(8,128)(2,1)} fusion(bf16[1536,4096]{1,0:T(8,128)(2,1)} %all-gather.3.cloned.1.call-done, bf16[448,1536]{1,0:T(8,128)(2,1)} %get-tuple-element.10, bf16[1,16,448]{2,1,0:T(8,128)(2,1)S(1)} %copy-done.9), kind=kOutput, calls=%fused_computation.13 | convolution fusion | flops 223502336 | bytes 14104576 | tf_op jit(solution)/shard_map/dot_general | solution.py:10
  309.4 78.8 %reduce-scatter.2.cloned.1.call-done = bf16[96,4096]{1,0:T(8,128)(2,1)} async-done(((bf16[1536,4096]{1,0:T(8,128)(2,1)}), bf16[96,4096]{1,0:T(8,128)(2,1)}) %reduce-scatter.2.cloned.1.call-update) | async-done | bytes 786448 | tf_op jit(solution)/shard_map/reduce_scatter | solution.py:170
  388.3 2.1 copy.60
  390.4 4.4 all-to-all-start.2
  394.8 0.3 all-reduce.5.cloned.1.call-start
  395.1 7.0 %fusion.5 = bf16[1,16,4096]{2,1,0:T(8,128)(2,1)} fusion(bf16[1536,16]{0,1:T(8,128)(2,1)S(1)} %convolution_convert_fusion.2, bf16[1536,4096]{1,0:T(8,128)(2,1)} %all-gather.5.cloned.1.call-done), kind=kOutput, calls=%fused_computation.15 | convolution fusion | flops 201457664 | bytes 12763136 | tf_op jit(solution)/shard_map/dot_general | solution.py:10
  402.1 1.1 fusion.25
  403.2 1.1 fusion.26
  404.3 1.1 fusion.24
  405.4 80.9 %all-reduce.5.cloned.1.call-done = (bf16[1,16,4096]{2,1,0:T(8,128)(2,1)}, bf16[1,16,4096]{2,1,0:T(8,128)(2,1)}, bf16[1,4096,16]{1,2,0:T(8,128)(2,1)}) async-done(((bf16[1,16,4096]{2,1,0:T(8,128)(2,1)}, bf16[1,16,4096]{2,1,0:T(8,128)(2,1)}, bf16[1,4096,16]{1,2,0:T(8,128)(2,1)}), (bf16[1,16,4096]{2,1,0:T(8,128)(2,1)}, bf16[1,16,4096]{2,1,0:T(8,128)(2,1)}, ...) | async-done | bytes 393232 | tf_op jit(solution)/shard_map/psum | solution.py:185
  486.3 1.6 broadcast_in_dim.57
  488.0 1.6 broadcast_in_dim.60
  489.6 1.6 broadcast_in_dim.64
  491.2 1.6 copy.59
  492.8 1.0 gather_fusion.3
  493.8 0.3 reshape.122
  494.1 1.3 reduce_sum.29
  (50 shorter events, 0.3 us)
Async XLA Ops:
  7.2 210.4 %copy-start = (bf16[1,4096,16]{1,2,0:T(8,128)(2,1)S(1)}, bf16[1,4096,16]{1,2,0:T(8,128)(2,1)}, u32[]{:S(2)}) copy-start(bf16[1,4096,16]{1,2,0:T(8,128)(2,1)} %param.25) | copy-start | bytes 393220
  7.2 118.5 %all-gather.5.cloned.1.call-start = ((), (), s32[]{:S(2)}) async-start(), calls=%async_computation.5 | async-start | bytes 13369344 | tf_op jit(solution)/shard_map/all_gather | solution.py:159
  16.7 19.5 %copy-start.11 = (f32[128,2]{0,1:T(2,128)S(1)}, f32[128,2]{0,1:T(2,128)}, u32[]{:S(2)}) copy-start(f32[128,2]{0,1:T(2,128)} %param.16) | copy-start | bytes 3076
  36.1 5.4 %copy-start.7 = (bf16[128,512]{1,0:T(8,128)(2,1)S(1)}, bf16[128,512]{1,0:T(8,128)(2,1)}, u32[]{:S(2)}) copy-start(bf16[128,512]{1,0:T(8,128)(2,1)} %param.14) | copy-start | bytes 393220
  36.2 181.3 %all-gather.3.cloned.1.call-start = ((), (), s32[]{:S(2)}) async-start(), calls=%async_computation.4 | async-start | bytes 13369344 | tf_op jit(solution)/shard_map/all_gather | solution.py:160
  44.3 81.4 %copy-start.5 = (bf16[1,16,4096]{2,1,0:T(8,128)(2,1)S(1)}, bf16[1,16,4096]{2,1,0:T(8,128)(2,1)}, u32[]{:S(2)}) copy-start(bf16[1,16,4096]{2,1,0:T(8,128)(2,1)} %param.20) | copy-start | bytes 393220
  61.2 327.1 %reduce-scatter.2.cloned.1.call-start = ((), (), s32[]{:S(2)}) async-start(), calls=%async_computation.6 | async-start | bytes 13369344 | tf_op jit(solution)/shard_map/reduce_scatter | solution.py:170
  125.7 8.2 %copy-start.2 = (bf16[1536,4096]{1,0:T(8,128)(2,1)S(1)}, bf16[1536,4096]{1,0:T(8,128)(2,1)}, u32[]{:S(2)}) copy-start(bf16[1536,4096]{1,0:T(8,128)(2,1)} %all-gather.5.cloned.1.call-done) | copy-start | bytes 37748740
  133.9 8.0 %copy-start.8 = (bf16[1,448,16]{1,2,0:T(8,128)(2,1)S(1)}, bf16[1,448,16]{1,2,0:T(8,128)(2,1)}, u32[]{:S(2)}) copy-start(bf16[1,448,16]{1,2,0:T(8,128)(2,1)} %param.21) | copy-start | bytes 43012
  217.5 8.1 %copy-start.12 = (bf16[1,448,4096]{2,1,0:T(8,128)(2,1)S(1)}, bf16[1,448,4096]{2,1,0:T(8,128)(2,1)}, u32[]{:S(2)}) copy-start(bf16[1,448,4096]{2,1,0:T(8,128)(2,1)} %param.19) | copy-start | bytes 11010052
  217.5 18.0 %slice-start = ((s8[12582912]{0:T(1024)(128)(4,1)}), s8[4194304]{0:T(1024)(128)(4,1)S(1)}, s32[]{:S(2)}) async-start(s8[12582912]{0:T(1024)(128)(4,1)} %bitcast.114), calls=%async_computation.8 | async-start | bytes 8388608
  225.6 9.3 %copy-start.9 = (bf16[1,16,448]{2,1,0:T(8,128)(2,1)S(1)}, bf16[1,16,448]{2,1,0:T(8,128)(2,1)}, u32[]{:S(2)}) copy-start(bf16[1,16,448]{2,1,0:T(8,128)(2,1)} %param.24) | copy-start | bytes 43012
  225.6 9.9 %slice-start.1 = ((s8[12582912]{0:T(1024)(128)(4,1)}), s8[4194304]{0:T(1024)(128)(4,1)S(1)}, s32[]{:S(2)}) async-start(s8[12582912]{0:T(1024)(128)(4,1)} %bitcast.114), calls=%async_computation.9 | async-start | bytes 8388608
  225.6 9.9 %slice-start.2 = ((s8[12582912]{0:T(1024)(128)(4,1)}), s8[4194304]{0:T(1024)(128)(4,1)S(1)}, s32[]{:S(2)}) async-start(s8[12582912]{0:T(1024)(128)(4,1)} %bitcast.114), calls=%async_computation.10 | async-start | bytes 8388608
  234.9 0.9 copy-start.6
  235.8 3.3 copy-start.13
  239.2 5.9 %copy-start.4 = (f32[448,1536]{1,0:T(8,128)S(1)}, f32[448,1536]{1,0:T(8,128)}, u32[]{:S(2)}) copy-start(f32[448,1536]{1,0:T(8,128)} %fusion.21) | copy-start | bytes 8257540
  239.2 5.9 %copy-start.10 = (bf16[1,448,16]{1,2,0:T(8,128)(2,1)S(1)}, bf16[1,448,16]{1,2,0:T(8,128)(2,1)}, u32[]{:S(2)}) copy-start(bf16[1,448,16]{1,2,0:T(8,128)(2,1)} %param.23) | copy-start | bytes 43012
  248.1 12.2 %copy-start.14 = (bf16[1,448,4096]{2,1,0:T(8,128)(2,1)S(1)}, bf16[1,448,4096]{2,1,0:T(8,128)(2,1)}, u32[]{:S(2)}) copy-start(bf16[1,448,4096]{2,1,0:T(8,128)(2,1)} %param.17) | copy-start | bytes 11010052
  390.4 100.9 %all-to-all-start.2 = ((bf16[96,8,512]{2,0,1:T(8,128)(2,1)}), bf16[96,8,512]{2,0,1:T(8,128)(2,1)}, u32[]{:S(2)}, u32[]{:S(2)}) async-start(bf16[96,8,512]{2,0,1:T(8,128)(2,1)} %bitcast.119), calls=%async_computation.3 | async-start | bytes 1572864 | tf_op jit(solution)/shard_map/all_to_all | solution.py:173
  394.8 91.6 %all-reduce.5.cloned.1.call-start = ((), (), s32[]{:S(2)}) async-start(), calls=%async_computation.7 | async-start | bytes 786432 | tf_op jit(solution)/shard_map/psum | solution.py:185
  402.1 2.2 copy-start.3
  492.8 2.6 copy-start.1
Sparse Core Ops, SparseCore 0:
  36.3 89.3 all-gather.4
  127.9 89.5 all-gather.2
  294.1 94.1 reduce-scatter.1
  402.2 84.0 all-reduce.4
where the time goes:
time: 507 us; the launch traced here: 502 us
  waiting for transfers between devices  297 us (59%)
  matrix products  120 us (24%)
  blocking collectives  34.1 us (7%)
  local copies, waits for them, and re-layouts  22.7 us (4%)
  between operations  14.4 us (3%)
  other arithmetic  8.74 us (2%)
  starting transfers between devices  5.36 us (1%)
    dot_general x20, matrix products, contract_pair(): lax.dot_general(left, right, (((left_axis,), (right_axis,)), ((), ())), p...  120 us
    psum x1, waiting for transfers between devices, local(): lax.psum(shared_slice[0].astype(jnp.bfloat16), 'dp').astype(jnp.float32)  80.9 us
    reduce_scatter x1, waiting for transfers between devices, local(): lax.psum_scatter(rows_part.astype(jnp.bfloat16), 'dp', scatter_dimension=...  78.8 us
    all_gather x1, waiting for transfers between devices, local(): lax.all_gather(recv_dy[0], 'dp', axis=0, tiled=True)  73.6 us
    all_gather x1, waiting for transfers between devices, local(): lax.all_gather(recv_x[0], 'dp', axis=0, tiled=True)  63.9 us
    all_to_all x1, blocking collectives, local(): lax.all_to_all(send_x, 'expert', split_axis=0, concat_axis=2, tiled=True)  18.4 us
    all_to_all x1, blocking collectives, local(): lax.all_to_all(send_dy, 'expert', split_axis=0, concat_axis=2, tiled=True)  15.7 us
  transfers between devices with their start and end apart: 5, of which 4 were waited for; matrix products, arithmetic and copies ran while one was open for 12% of the time, Pallas kernels for 0%

commit v1 on v0

--- a/solution.py
+++ b/solution.py
@@ -4,6 +4,24 @@
 from jax.sharding import PartitionSpec as P
 
 ADAPTER_SCALE = 2.0
+
+
+def collect(value, axis, dim):
+    ways, here, hop = (lax.axis_size(axis), lax.axis_index(axis), value.shape[dim])
+    shape = [n * ways if d == dim else n for d, n in enumerate(value.shape)]
+    full = lax.dynamic_update_slice_in_dim(
+        jnp.zeros(shape, value.dtype), value, here * hop, axis=dim
+    )
+    going_up = going_down = value
+    for far in range(1, ways // 2 + 1):
+        going_up = lax.ppermute(going_up, axis, [(d, (d + 1) % ways) for d in range(ways)])
+        full = lax.dynamic_update_slice_in_dim(full, going_up, (here - far) % ways * hop, axis=dim)
+        if 2 * far < ways:
+            going_down = lax.ppermute(going_down, axis, [(d, (d - 1) % ways) for d in range(ways)])
+            full = lax.dynamic_update_slice_in_dim(
+                full, going_down, (here + far) % ways * hop, axis=dim
+            )
+    return full
 
 
 def contract_pair(left, right, left_axis, right_axis):
@@ -156,9 +174,7 @@
         lax.all_to_all(send_dy, "expert", split_axis=0, concat_axis=2, tiled=True),
     )
     gradient_rows_out, shared_slice, owned_slice = rows_backward_pass(
-        lax.all_gather(recv_x[0], "dp", axis=0, tiled=True),
-        lax.all_gather(recv_dy[0], "dp", axis=0, tiled=True),
-        params,
+        collect(recv_x[0], "dp", 0), lax.all_gather(recv_dy[0], "dp", axis=0, tiled=True), params
     )
     rows_part = gradient_rows_out
     totals = (

time: 507 us -> 591 us (1.17)
  starting transfers between devices: 5.36 us -> 43.7 us
  local copies, waits for them, and re-layouts: 22.7 us -> 43.8 us
  waiting for transfers between devices: 297 us -> 310 us
  matrix products: 120 us -> 126 us
    ppermute x0 -> x15, waiting for transfers between devices: none -> 153 us  [the longest x7 121 us: collect(): lax.ppermute(going_down, axis, [(d, (d - 1) % ways) for d in range(ways)])]
    all_gather x1, waiting for transfers between devices: 73.6 us -> 0.01 us  [local(): lax.all_gather(recv_dy[0], 'dp', axis=0, tiled=True)]
    all_gather x1 -> x0, waiting for transfers between devices: 63.9 us -> none  [local(): lax.all_gather(recv_x[0], 'dp', axis=0, tiled=True)]
    ppermute x0 -> x15, starting transfers between devices: none -> 38.9 us  [the longest x7 38.5 us: collect(): lax.ppermute(going_down, axis, [(d, (d - 1) % ways) for d in range(ways)])]
    dynamic_update_slice x0 -> x16, local copies, waits for them, and re-layouts: none -> 15.3 us  [the longest x8 7.59 us: collect(): lax.dynamic_update_slice_in_dim(full, going_up, (here - far) % ways * hop...]
    dot_general x20, matrix products: 120 us -> 126 us  [contract_pair(): lax.dot_general(left, right, (((left_axis,), (right_axis,)), ((), ())), p...]
    broadcast_in_dim x0 -> x1, local copies, waits for them, and re-layouts: none -> 6.11 us  [collect(): jnp.zeros(shape, value.dtype)]
  transfers between devices with their start and end apart: 5 -> 19, of which waited for: 4 -> 10; matrix products, arithmetic and copies ran while one was open for 12% -> 13% of each run, Pallas kernels for 0% -> 0%
where the time goes in v1:
time: 591 us; the launch traced here: 581 us
  waiting for transfers between devices  310 us (52%)
  matrix products  126 us (21%)
  local copies, waits for them, and re-layouts  43.8 us (7%)
  starting transfers between devices  43.7 us (7%)
  blocking collectives  34.1 us (6%)
  between operations  14.5 us (2%)
  other arithmetic  8.75 us (1%)
    dot_general x20, matrix products, contract_pair(): lax.dot_general(left, right, (((left_axis,), (right_axis,)), ((), ())), p...  126 us
    ppermute x7, waiting for transfers between devices, collect(): lax.ppermute(going_down, axis, [(d, (d - 1) % ways) for d in range(ways)])  121 us
    psum x1, waiting for transfers between devices, local(): lax.psum(shared_slice[0].astype(jnp.bfloat16), 'dp').astype(jnp.float32)  79.6 us
    reduce_scatter x1, waiting for transfers between devices, local(): lax.psum_scatter(rows_part.astype(jnp.bfloat16), 'dp', scatter_dimension=...  77.3 us
    ppermute x7, starting transfers between devices, collect(): lax.ppermute(going_down, axis, [(d, (d - 1) % ways) for d in range(ways)])  38.5 us
    ppermute x8, waiting for transfers between devices, collect(): lax.ppermute(going_up, axis, [(d, (d + 1) % ways) for d in range(ways)])  32.4 us
    all_to_all x1, blocking collectives, local(): lax.all_to_all(send_dy, 'expert', split_axis=0, concat_axis=2, tiled=True)  18.4 us
    all_to_all x1, blocking collectives, local(): lax.all_to_all(send_x, 'expert', split_axis=0, concat_axis=2, tiled=True)  15.7 us
  transfers between devices with their start and end apart: 19, of which 10 were waited for; matrix products, arithmetic and copies ran while one was open for 13% of the time, Pallas kernels for 0%

profile of v1, /device:TPU:0, one launch (start us, length us, event | category | flops | bytes accessed | tf_op | source)
XLA Modules:
  0.0 581.0 jit_solution(491482461115987259)
XLA Ops:
  11.2 1.4 scatter_custom_fusion.1
  12.6 1.4 scatter_custom_fusion
  14.1 5.0 gather_fusion
  19.2 2.7 gather_fusion.1
  22.1 18.4 %all_to_all.35 = bf16[8,96,512]{2,1,0:T(8,128)(2,1)S(1)} all-to-all(bf16[8,96,512]{2,1,0:T(8,128)(2,1)S(1)} %fusion.31), channel_id=1, replica_groups=mesh['dp'=16,'expert'=8] {'expert'}, dimensions={0} | all-to-all | bytes 1572864 | tf_op jit(solution)/shard_map/all_to_all | solution.py:174
  40.5 1.0 copy.53
  41.6 2.7 gather_fusion.2
  44.3 15.7 %all_to_all.36 = bf16[8,96,512]{2,1,0:T(8,128)(2,1)S(1)} all-to-all(bf16[8,96,512]{2,1,0:T(8,128)(2,1)S(1)} %bitcast.126), channel_id=1, replica_groups=mesh['dp'=16,'expert'=8] {'expert'}, dimensions={0} | all-to-all | bytes 1572864 | tf_op jit(solution)/shard_map/all_to_all | solution.py:173
  60.1 5.3 collective-permute-start.1
  65.3 6.1 %broadcast_in_dim.58 = bf16[1536,4096]{1,0:T(8,128)(2,1)} broadcast(bf16[]{:T(256)} %constant.123.clone.1), dimensions={} | broadcast | bytes 12582914 | tf_op jit(solution)/shard_map/broadcast_in_dim | solution.py:13
  71.4 1.0 constant_dynamic-update-slice_fusion.15
  72.5 12.2 %collective-permute-done.1 = bf16[96,4096]{1,0:T(8,128)(2,1)S(1)} collective-permute-done((bf16[96,4096]{1,0:T(8,128)(2,1)S(1)}, bf16[96,4096]{1,0:T(8,128)(2,1)S(1)}, u32[]{:S(2)}, u32[]{:S(2)}) %collective-permute-start.1) | collective-permute-done | bytes 786464 | tf_op jit(solution)/shard_map/ppermute | solution.py:20
  84.7 4.2 collective-permute-start.3
  88.9 0.9 constant_dynamic-update-slice_fusion.14
  90.8 28.0 %collective-permute-done.3 = bf16[96,4096]{1,0:T(8,128)(2,1)S(1)} collective-permute-done((bf16[96,4096]{1,0:T(8,128)(2,1)S(1)}, bf16[96,4096]{1,0:T(8,128)(2,1)S(1)}, u32[]{:S(2)}, u32[]{:S(2)}) %collective-permute-start.3) | collective-permute-done | bytes 786464 | tf_op jit(solution)/shard_map/ppermute | solution.py:20
  118.8 5.8 collective-permute-start.5
  126.4 31.0 %collective-permute-done.5 = bf16[96,4096]{1,0:T(8,128)(2,1)S(1)} collective-permute-done((bf16[96,4096]{1,0:T(8,128)(2,1)S(1)}, bf16[96,4096]{1,0:T(8,128)(2,1)S(1)}, u32[]{:S(2)}, u32[]{:S(2)}) %collective-permute-start.5) | collective-permute-done | bytes 786464 | tf_op jit(solution)/shard_map/ppermute | solution.py:20
  157.4 5.8 collective-permute-start.7
  163.2 1.0 constant_dynamic-update-slice_fusion.10
  164.2 1.0 constant_dynamic-update-slice_fusion.9
  165.2 24.4 %collective-permute-done.7 = bf16[96,4096]{1,0:T(8,128)(2,1)S(1)} collective-permute-done((bf16[96,4096]{1,0:T(8,128)(2,1)S(1)}, bf16[96,4096]{1,0:T(8,128)(2,1)S(1)}, u32[]{:S(2)}, u32[]{:S(2)}) %collective-permute-start.7) | collective-permute-done | bytes 786464 | tf_op jit(solution)/shard_map/ppermute | solution.py:20
  189.6 5.8 %collective-permute-start.9 = (bf16[96,4096]{1,0:T(8,128)(2,1)S(1)}, bf16[96,4096]{1,0:T(8,128)(2,1)S(1)}, u32[]{:S(2)}, u32[]{:S(2)}) collective-permute-start(bf16[96,4096]{1,0:T(8,128)(2,1)S(1)} %collective-permute-done.7), channel_id=1, source_target_pairs={{0,120},{8,0},{16,8},{24,16},{32,24},{40,32},{48,40},{56,48},{64,5... | collective-permute-start | bytes 2359304 | tf_op jit(solution)/shard_map/ppermute | solution.py:20
  195.4 0.9 constant_dynamic-update-slice_fusion.8
  196.3 1.0 constant_dynamic-update-slice_fusion.7
  197.3 13.0 %collective-permute-done.9 = bf16[96,4096]{1,0:T(8,128)(2,1)S(1)} collective-permute-done((bf16[96,4096]{1,0:T(8,128)(2,1)S(1)}, bf16[96,4096]{1,0:T(8,128)(2,1)S(1)}, u32[]{:S(2)}, u32[]{:S(2)}) %collective-permute-start.9) | collective-permute-done | bytes 786464 | tf_op jit(solution)/shard_map/ppermute | solution.py:20
  210.3 5.8 collective-permute-start.11
  216.1 1.0 constant_dynamic-update-slice_fusion.6
  217.1 1.0 constant_dynamic-update-slice_fusion.5
  218.1 12.0 %collective-permute-done.11 = bf16[96,4096]{1,0:T(8,128)(2,1)S(1)} collective-permute-done((bf16[96,4096]{1,0:T(8,128)(2,1)S(1)}, bf16[96,4096]{1,0:T(8,128)(2,1)S(1)}, u32[]{:S(2)}, u32[]{:S(2)}) %collective-permute-start.11) | collective-permute-done | bytes 786464 | tf_op jit(solution)/shard_map/ppermute | solution.py:20
  230.0 5.8 collective-permute-start.13
  235.8 0.9 constant_dynamic-update-slice_fusion.4
  236.8 0.9 constant_dynamic-update-slice_fusion.3
  237.7 16.7 %collective-permute-done.12 = bf16[96,4096]{1,0:T(8,128)(2,1)S(1)} collective-permute-done((bf16[96,4096]{1,0:T(8,128)(2,1)S(1)}, bf16[96,4096]{1,0:T(8,128)(2,1)S(1)}, u32[]{:S(2)}, u32[]{:S(2)}) %collective-permute-start.12) | collective-permute-done | bytes 786464 | tf_op jit(solution)/shard_map/ppermute | solution.py:17
  254.7 0.9 constant_dynamic-update-slice_fusion.2
  255.7 1.0 constant_dynamic-update-slice_fusion.1
  256.6 15.7 %collective-permute-done.14 = bf16[96,4096]{1,0:T(8,128)(2,1)S(1)} collective-permute-done((bf16[96,4096]{1,0:T(8,128)(2,1)S(1)}, bf16[96,4096]{1,0:T(8,128)(2,1)S(1)}, u32[]{:S(2)}, u32[]{:S(2)}) %collective-permute-start.14) | collective-permute-done | bytes 786464 | tf_op jit(solution)/shard_map/ppermute | solution.py:17
  272.4 1.0 constant_dynamic-update-slice_fusion
  273.3 8.1 %convolution_convert_fusion.4 = bf16[1536,16]{0,1:T(8,128)(2,1)S(1)} fusion(bf16[1536,4096]{1,0:T(8,128)(2,1)} %constant_dynamic-update-slice_fusion, bf16[1,16,4096]{2,1,0:T(8,128)(2,1)S(1)} %copy-done.5), kind=kOutput, calls=%fused_computation.44 | convolution fusion | flops 201351168 | bytes 12763136 | tf_op jit(solution)/shard_map/dot_general | solution.py:28
  281.4 2.1 convolution_multiply_fusion.4
  283.6 3.3 convolution_convert_fusion.3
  287.5 7.4 %fusion.23 = f32[448,1536]{1,0:T(8,128)} fusion(f32[1536,448]{0,1:T(8,128)S(1)} %convolution_multiply_fusion.3, bf16[1536,4096]{1,0:T(8,128)(2,1)S(1)} %copy-done.2, bf16[1,448,4096]{2,1,0:T(8,128)(2,1)S(1)} %copy-done.12), kind=kOutput, calls=%fused_computation.32 | convolution fusion | flops 5637832704 | bytes 21757952 | tf_op jit(solution)/shard_map/dot_general | solution.py:28
  294.9 8.2 %convolution_convert_fusion.5 = bf16[1536,16]{0,1:T(8,128)(2,1)S(1)} fusion(bf16[1536,4096]{1,0:T(8,128)(2,1)} %all-gather.2.cloned.1.call-done, bf16[1,4096,16]{1,2,0:T(8,128)(2,1)S(1)} %copy-done), kind=kOutput, calls=%fused_computation.45 | convolution fusion | flops 201351168 | bytes 12763136 | tf_op jit(solution)/shard_map/dot_general | solution.py:28
  303.2 9.3 %fusion.14 = f32[1536,448]{0,1:T(8,128)S(1)} fusion(bf16[1536,4096]{1,0:T(8,128)(2,1)} %all-gather.2.cloned.1.call-done, bf16[1,448,4096]{2,1,0:T(8,128)(2,1)S(1)} %copy-done.11), kind=kOutput, calls=%fused_computation.24 | convolution fusion | flops 5637144576 | bytes 19005440 | tf_op jit(solution)/shard_map/dot_general | solution.py:28
  313.1 1.2 copy-done.3
  314.3 12.0 %multiply_convert_fusion = (bf16[448,1536]{1,0:T(8,128)(2,1)}, bf16[448,1536]{1,0:T(8,128)(2,1)S(1)}, bf16[448,1536]{1,0:T(8,128)(2,1)S(1)}) fusion(f32[448,1536]{1,0:T(8,128)} %fusion.23, f32[448,1536]{1,0:T(8,128)S(1)} %fusion.29, f32[1536,448]{0,1:T(8,128)S(1)} %copy-done.3, bf16[1536,4096]{1,0:T(8,128)(2,1)S(1)} %bitcast.123, ...), kind=kOutput, calls=%fused_computation.35 | convolution fusion | flops 5648154624 | bytes 28639232 | tf_op jit(solution)/shard_map/dot_general | solution.py:28
  326.6 13.9 %fusion.10 = f32[1536,4096]{1,0:T(8,128)} fusion(bf16[448,1536]{1,0:T(8,128)(2,1)S(1)} %get-tuple-element.12, bf16[1,448,4096]{2,1,0:T(8,128)(2,1)} %param.18), kind=kOutput, calls=%fused_computation.20 | convolution fusion | flops 5637144576 | bytes 30212096 | tf_op jit(solution)/shard_map/dot_general | solution.py:28
  340.8 12.0 %fusion.6 = f32[1536,4096]{1,0:T(8,128)} fusion(bf16[448,1536]{1,0:T(8,128)(2,1)S(1)} %get-tuple-element.11, bf16[1,448,4096]{2,1,0:T(8,128)(2,1)S(1)} %copy-done.13), kind=kOutput, calls=%fused_computation.16 | convolution fusion | flops 5637144576 | bytes 30212096 | tf_op jit(solution)/shard_map/dot_general | solution.py:28
  352.7 21.9 %add_convert_fusion = bf16[1536,4096]{1,0:T(8,128)(2,1)} fusion(f32[1536,4096]{1,0:T(8,128)} %fusion.6, f32[1536,4096]{1,0:T(8,128)} %fusion.10, bf16[16,4096]{1,0:T(8,128)(2,1)S(1)} %bitcast.138, bf16[16,4096]{1,0:T(8,128)(2,1)S(1)} %bitcast.137, bf16[16,1536]{1,0:T(8,128)(2,1)S(1)} %bitcast.136, bf16[16,1536]{1,0:T(8,128)(2,1)S(1)} %bitcast.135), kind=kOutput, calls=%fused_computation.6 | convolution fusion | flops 428539904 | bytes 63275008 | tf_op jit(solution)/shard_map/dot_general | solution.py:28
  374.9 7.0 %fusion.4 = bf16[1,16,4096]{2,1,0:T(8,128)(2,1)} fusion(bf16[1536,16]{0,1:T(8,128)(2,1)S(1)} %convolution_convert_fusion.1, bf16[1536,4096]{1,0:T(8,128)(2,1)} %constant_dynamic-update-slice_fusion), kind=kOutput, calls=%fused_computation.14 | convolution fusion | flops 201457664 | bytes 12763136 | tf_op jit(solution)/shard_map/dot_general | solution.py:28
  381.9 7.6 %fusion.3 = bf16[1,4096,16]{1,2,0:T(8,128)(2,1)} fusion(bf16[1536,4096]{1,0:T(8,128)(2,1)} %all-gather.2.cloned.1.call-done, bf16[448,1536]{1,0:T(8,128)(2,1)} %get-tuple-element.10, bf16[1,16,448]{2,1,0:T(8,128)(2,1)S(1)} %copy-done.10), kind=kOutput, calls=%fused_computation.13 | convolution fusion | flops 223502336 | bytes 14104576 | tf_op jit(solution)/shard_map/dot_general | solution.py:28
  389.5 77.3 %reduce-scatter.2.cloned.1.call-done = bf16[96,4096]{1,0:T(8,128)(2,1)} async-done(((bf16[1536,4096]{1,0:T(8,128)(2,1)}), bf16[96,4096]{1,0:T(8,128)(2,1)}) %reduce-scatter.2.cloned.1.call-update) | async-done | bytes 786448 | tf_op jit(solution)/shard_map/reduce_scatter | solution.py:186
  466.8 2.1 copy.60
  468.9 4.4 all-to-all-start.2
  473.6 7.0 %fusion.5 = bf16[1,16,4096]{2,1,0:T(8,128)(2,1)} fusion(bf16[1536,16]{0,1:T(8,128)(2,1)S(1)} %convolution_convert_fusion.2, bf16[1536,4096]{1,0:T(8,128)(2,1)} %constant_dynamic-update-slice_fusion), kind=kOutput, calls=%fused_computation.15 | convolution fusion | flops 201457664 | bytes 12763136 | tf_op jit(solution)/shard_map/dot_general | solution.py:28
  480.6 1.1 fusion.33
  481.7 1.1 fusion.34
  482.8 2.4 fusion.32
  485.3 79.6 %all-reduce.5.cloned.1.call-done = (bf16[1,16,4096]{2,1,0:T(8,128)(2,1)}, bf16[1,16,4096]{2,1,0:T(8,128)(2,1)}, bf16[1,4096,16]{1,2,0:T(8,128)(2,1)}) async-done(((bf16[1,16,4096]{2,1,0:T(8,128)(2,1)}, bf16[1,16,4096]{2,1,0:T(8,128)(2,1)}, bf16[1,4096,16]{1,2,0:T(8,128)(2,1)}), (bf16[1,16,4096]{2,1,0:T(8,128)(2,1)}, bf16[1,16,4096]{2,1,0:T(8,128)(2,1)}, ...) | async-done | bytes 393232 | tf_op jit(solution)/shard_map/psum | solution.py:201
  564.9 1.6 broadcast_in_dim.61
  566.5 1.6 broadcast_in_dim.64
  568.2 1.6 broadcast_in_dim.68
  569.8 1.6 copy.59
  571.4 1.0 gather_fusion.3
  572.7 1.3 reduce_sum.29
  (92 shorter events, 10.3 us)
Async XLA Ops:
  7.2 287.8 %copy-start = (bf16[1,4096,16]{1,2,0:T(8,128)(2,1)S(1)}, bf16[1,4096,16]{1,2,0:T(8,128)(2,1)}, u32[]{:S(2)}) copy-start(bf16[1,4096,16]{1,2,0:T(8,128)(2,1)} %param.25) | copy-start | bytes 393220
  7.2 12.0 %copy-start.6 = (bf16[128,512]{1,0:T(8,128)(2,1)S(1)}, bf16[128,512]{1,0:T(8,128)(2,1)}, u32[]{:S(2)}) copy-start(bf16[128,512]{1,0:T(8,128)(2,1)} %param.14) | copy-start | bytes 393220
  7.2 287.7 %all-gather.2.cloned.1.call-start = ((), (), s32[]{:S(2)}) async-start(), calls=%async_computation.4 | async-start | bytes 13369344 | tf_op jit(solution)/shard_map/all_gather | solution.py:177
  21.8 19.8 %copy-start.7 = (bf16[128,512]{1,0:T(8,128)(2,1)S(1)}, bf16[128,512]{1,0:T(8,128)(2,1)}, u32[]{:S(2)}) copy-start(bf16[128,512]{1,0:T(8,128)(2,1)} %param.13) | copy-start | bytes 393220
  41.5 425.2 %reduce-scatter.2.cloned.1.call-start = ((), (), s32[]{:S(2)}) async-start(), calls=%async_computation.5 | async-start | bytes 13369344 | tf_op jit(solution)/shard_map/reduce_scatter | solution.py:186
  60.1 24.6 %collective-permute-start.1 = (bf16[96,4096]{1,0:T(8,128)(2,1)S(1)}, bf16[96,4096]{1,0:T(8,128)(2,1)S(1)}, u32[]{:S(2)}, u32[]{:S(2)}) collective-permute-start(bf16[96,4096]{1,0:T(8,128)(2,1)S(1)} %bitcast.128), channel_id=1, source_target_pairs={{0,120},{8,0},{16,8},{24,16},{32,24},{40,32},{48,40},{56,48},{64,5... | collective-permute-start | bytes 2359304 | tf_op jit(solution)/shard_map/ppermute | solution.py:20
  65.3 23.5 %collective-permute-start = (bf16[96,4096]{1,0:T(8,128)(2,1)S(1)}, bf16[96,4096]{1,0:T(8,128)(2,1)S(1)}, u32[]{:S(2)}, u32[]{:S(2)}) collective-permute-start(bf16[96,4096]{1,0:T(8,128)(2,1)S(1)} %bitcast.129), channel_id=1, source_target_pairs={{0,8},{8,16},{16,24},{24,32},{32,40},{40,48},{48,56},{56,64},{64,7... | collective-permute-start | bytes 2359304 | tf_op jit(solution)/shard_map/ppermute | solution.py:17
  84.7 34.1 %collective-permute-start.3 = (bf16[96,4096]{1,0:T(8,128)(2,1)S(1)}, bf16[96,4096]{1,0:T(8,128)(2,1)S(1)}, u32[]{:S(2)}, u32[]{:S(2)}) collective-permute-start(bf16[96,4096]{1,0:T(8,128)(2,1)S(1)} %collective-permute-done.1), channel_id=1, source_target_pairs={{0,120},{8,0},{16,8},{24,16},{32,24},{40,32},{48,40},{56,48},{64,5... | collective-permute-start | bytes 2359304 | tf_op jit(solution)/shard_map/ppermute | solution.py:20
  88.9 35.7 %collective-permute-start.2 = (bf16[96,4096]{1,0:T(8,128)(2,1)S(1)}, bf16[96,4096]{1,0:T(8,128)(2,1)S(1)}, u32[]{:S(2)}, u32[]{:S(2)}) collective-permute-start(bf16[96,4096]{1,0:T(8,128)(2,1)S(1)} %collective-permute-done), channel_id=1, source_target_pairs={{0,8},{8,16},{16,24},{24,32},{32,40},{40,48},{48,56},{56,64},{64,7... | collective-permute-start | bytes 2359304 | tf_op jit(solution)/shard_map/ppermute | solution.py:17
  118.8 38.7 %collective-permute-start.5 = (bf16[96,4096]{1,0:T(8,128)(2,1)S(1)}, bf16[96,4096]{1,0:T(8,128)(2,1)S(1)}, u32[]{:S(2)}, u32[]{:S(2)}) collective-permute-start(bf16[96,4096]{1,0:T(8,128)(2,1)S(1)} %collective-permute-done.3), channel_id=1, source_target_pairs={{0,120},{8,0},{16,8},{24,16},{32,24},{40,32},{48,40},{56,48},{64,5... | collective-permute-start | bytes 2359304 | tf_op jit(solution)/shard_map/ppermute | solution.py:20
  124.6 38.7 %collective-permute-start.4 = (bf16[96,4096]{1,0:T(8,128)(2,1)S(1)}, bf16[96,4096]{1,0:T(8,128)(2,1)S(1)}, u32[]{:S(2)}, u32[]{:S(2)}) collective-permute-start(bf16[96,4096]{1,0:T(8,128)(2,1)S(1)} %collective-permute-done.2), channel_id=1, source_target_pairs={{0,8},{8,16},{16,24},{24,32},{32,40},{40,48},{48,56},{56,64},{64,7... | collective-permute-start | bytes 2359304 | tf_op jit(solution)/shard_map/ppermute | solution.py:17
  157.4 32.1 %collective-permute-start.7 = (bf16[96,4096]{1,0:T(8,128)(2,1)S(1)}, bf16[96,4096]{1,0:T(8,128)(2,1)S(1)}, u32[]{:S(2)}, u32[]{:S(2)}) collective-permute-start(bf16[96,4096]{1,0:T(8,128)(2,1)S(1)} %collective-permute-done.5), channel_id=1, source_target_pairs={{0,120},{8,0},{16,8},{24,16},{32,24},{40,32},{48,40},{56,48},{64,5... | collective-permute-start | bytes 2359304 | tf_op jit(solution)/shard_map/ppermute | solution.py:20
  163.2 32.2 %collective-permute-start.6 = (bf16[96,4096]{1,0:T(8,128)(2,1)S(1)}, bf16[96,4096]{1,0:T(8,128)(2,1)S(1)}, u32[]{:S(2)}, u32[]{:S(2)}) collective-permute-start(bf16[96,4096]{1,0:T(8,128)(2,1)S(1)} %collective-permute-done.4), channel_id=1, source_target_pairs={{0,8},{8,16},{16,24},{24,32},{32,40},{40,48},{48,56},{56,64},{64,7... | collective-permute-start | bytes 2359304 | tf_op jit(solution)/shard_map/ppermute | solution.py:17
  189.6 20.7 %collective-permute-start.9 = (bf16[96,4096]{1,0:T(8,128)(2,1)S(1)}, bf16[96,4096]{1,0:T(8,128)(2,1)S(1)}, u32[]{:S(2)}, u32[]{:S(2)}) collective-permute-start(bf16[96,4096]{1,0:T(8,128)(2,1)S(1)} %collective-permute-done.7), channel_id=1, source_target_pairs={{0,120},{8,0},{16,8},{24,16},{32,24},{40,32},{48,40},{56,48},{64,5... | collective-permute-start | bytes 2359304 | tf_op jit(solution)/shard_map/ppermute | solution.py:20
  195.4 20.7 %collective-permute-start.8 = (bf16[96,4096]{1,0:T(8,128)(2,1)S(1)}, bf16[96,4096]{1,0:T(8,128)(2,1)S(1)}, u32[]{:S(2)}, u32[]{:S(2)}) collective-permute-start(bf16[96,4096]{1,0:T(8,128)(2,1)S(1)} %collective-permute-done.6), channel_id=1, source_target_pairs={{0,8},{8,16},{16,24},{24,32},{32,40},{40,48},{48,56},{56,64},{64,7... | collective-permute-start | bytes 2359304 | tf_op jit(solution)/shard_map/ppermute | solution.py:17
  210.3 19.8 %collective-permute-start.11 = (bf16[96,4096]{1,0:T(8,128)(2,1)S(1)}, bf16[96,4096]{1,0:T(8,128)(2,1)S(1)}, u32[]{:S(2)}, u32[]{:S(2)}) collective-permute-start(bf16[96,4096]{1,0:T(8,128)(2,1)S(1)} %collective-permute-done.9), channel_id=1, source_target_pairs={{0,120},{8,0},{16,8},{24,16},{32,24},{40,32},{48,40},{56,48},{64,5... | collective-permute-start | bytes 2359304 | tf_op jit(solution)/shard_map/ppermute | solution.py:20
  216.1 19.8 %collective-permute-start.10 = (bf16[96,4096]{1,0:T(8,128)(2,1)S(1)}, bf16[96,4096]{1,0:T(8,128)(2,1)S(1)}, u32[]{:S(2)}, u32[]{:S(2)}) collective-permute-start(bf16[96,4096]{1,0:T(8,128)(2,1)S(1)} %collective-permute-done.8), channel_id=1, source_target_pairs={{0,8},{8,16},{16,24},{24,32},{32,40},{40,48},{48,56},{56,64},{64,7... | collective-permute-start | bytes 2359304 | tf_op jit(solution)/shard_map/ppermute | solution.py:17
  218.1 55.2 %copy-start.5 = (bf16[1,16,4096]{2,1,0:T(8,128)(2,1)S(1)}, bf16[1,16,4096]{2,1,0:T(8,128)(2,1)}, u32[]{:S(2)}) copy-start(bf16[1,16,4096]{2,1,0:T(8,128)(2,1)} %param.22) | copy-start | bytes 393220
  230.0 25.7 %collective-permute-start.13 = (bf16[96,4096]{1,0:T(8,128)(2,1)S(1)}, bf16[96,4096]{1,0:T(8,128)(2,1)S(1)}, u32[]{:S(2)}, u32[]{:S(2)}) collective-permute-start(bf16[96,4096]{1,0:T(8,128)(2,1)S(1)} %collective-permute-done.11), channel_id=1, source_target_pairs={{0,120},{8,0},{16,8},{24,16},{32,24},{40,32},{48,40},{56,48},{64,5... | collective-permute-start | bytes 2359304 | tf_op jit(solution)/shard_map/ppermute | solution.py:20
  235.8 18.6 %collective-permute-start.12 = (bf16[96,4096]{1,0:T(8,128)(2,1)S(1)}, bf16[96,4096]{1,0:T(8,128)(2,1)S(1)}, u32[]{:S(2)}, u32[]{:S(2)}) collective-permute-start(bf16[96,4096]{1,0:T(8,128)(2,1)S(1)} %collective-permute-done.10), channel_id=1, source_target_pairs={{0,8},{8,16},{16,24},{24,32},{32,40},{40,48},{48,56},{56,64},{64,7... | collective-permute-start | bytes 2359304 | tf_op jit(solution)/shard_map/ppermute | solution.py:17
  254.4 18.0 %collective-permute-start.14 = (bf16[96,4096]{1,0:T(8,128)(2,1)S(1)}, bf16[96,4096]{1,0:T(8,128)(2,1)S(1)}, u32[]{:S(2)}, u32[]{:S(2)}) collective-permute-start(bf16[96,4096]{1,0:T(8,128)(2,1)S(1)} %collective-permute-done.12), channel_id=1, source_target_pairs={{0,8},{8,16},{16,24},{24,32},{32,40},{40,48},{48,56},{56,64},{64,7... | collective-permute-start | bytes 2359304 | tf_op jit(solution)/shard_map/ppermute | solution.py:17
  273.3 8.1 %copy-start.8 = (bf16[1,448,16]{1,2,0:T(8,128)(2,1)S(1)}, bf16[1,448,16]{1,2,0:T(8,128)(2,1)}, u32[]{:S(2)}) copy-start(bf16[1,448,16]{1,2,0:T(8,128)(2,1)} %param.23) | copy-start | bytes 43012
  273.3 10.2 %copy-start.2 = (bf16[1536,4096]{1,0:T(8,128)(2,1)S(1)}, bf16[1536,4096]{1,0:T(8,128)(2,1)}, u32[]{:S(2)}) copy-start(bf16[1536,4096]{1,0:T(8,128)(2,1)} %constant_dynamic-update-slice_fusion) | copy-start | bytes 37748740
  273.3 10.2 %copy-start.4 = (bf16[1,16,4096]{2,1,0:T(8,128)(2,1)S(1)}, bf16[1,16,4096]{2,1,0:T(8,128)(2,1)}, u32[]{:S(2)}) copy-start(bf16[1,16,4096]{2,1,0:T(8,128)(2,1)} %param.20) | copy-start | bytes 393220
  283.6 3.4 copy-start.9
  283.6 3.9 copy-start.12
  294.9 8.2 %copy-start.11 = (bf16[1,448,4096]{2,1,0:T(8,128)(2,1)S(1)}, bf16[1,448,4096]{2,1,0:T(8,128)(2,1)}, u32[]{:S(2)}) copy-start(bf16[1,448,4096]{2,1,0:T(8,128)(2,1)} %param.19) | copy-start | bytes 11010052
  294.9 18.2 %slice-start = ((s8[12582912]{0:T(1024)(128)(4,1)}), s8[4194304]{0:T(1024)(128)(4,1)S(1)}, s32[]{:S(2)}) async-start(s8[12582912]{0:T(1024)(128)(4,1)} %bitcast.122), calls=%async_computation.7 | async-start | bytes 8388608
  303.2 9.3 %copy-start.10 = (bf16[1,16,448]{2,1,0:T(8,128)(2,1)S(1)}, bf16[1,16,448]{2,1,0:T(8,128)(2,1)}, u32[]{:S(2)}) copy-start(bf16[1,16,448]{2,1,0:T(8,128)(2,1)} %param.24) | copy-start | bytes 43012
  303.2 9.9 %slice-start.1 = ((s8[12582912]{0:T(1024)(128)(4,1)}), s8[4194304]{0:T(1024)(128)(4,1)S(1)}, s32[]{:S(2)}) async-start(s8[12582912]{0:T(1024)(128)(4,1)} %bitcast.122), calls=%async_computation.8 | async-start | bytes 8388608
  303.2 9.9 %slice-start.2 = ((s8[12582912]{0:T(1024)(128)(4,1)}), s8[4194304]{0:T(1024)(128)(4,1)S(1)}, s32[]{:S(2)}) async-start(s8[12582912]{0:T(1024)(128)(4,1)} %bitcast.122), calls=%async_computation.9 | async-start | bytes 8388608
  312.5 1.8 copy-start.3
  326.6 14.2 %copy-start.13 = (bf16[1,448,4096]{2,1,0:T(8,128)(2,1)S(1)}, bf16[1,448,4096]{2,1,0:T(8,128)(2,1)}, u32[]{:S(2)}) copy-start(bf16[1,448,4096]{2,1,0:T(8,128)(2,1)} %param.17) | copy-start | bytes 11010052
  468.9 100.9 %all-to-all-start.2 = ((bf16[96,8,512]{2,0,1:T(8,128)(2,1)}), bf16[96,8,512]{2,0,1:T(8,128)(2,1)}, u32[]{:S(2)}, u32[]{:S(2)}) async-start(bf16[96,8,512]{2,0,1:T(8,128)(2,1)} %bitcast.131), calls=%async_computation.3 | async-start | bytes 1572864 | tf_op jit(solution)/shard_map/all_to_all | solution.py:189
  473.3 91.6 %all-reduce.5.cloned.1.call-start = ((), (), s32[]{:S(2)}) async-start(), calls=%async_computation.6 | async-start | bytes 786432 | tf_op jit(solution)/shard_map/psum | solution.py:201
  569.8 4.2 copy-start.1
Sparse Core Ops, SparseCore 0:
  41.7 149.6 all-gather.1
  374.7 92.0 reduce-scatter.1
  480.7 84.1 all-reduce.4
